TPU v7x, 512 devices: a whole 4x8x8 slice. The times are simulated.
512 devices in a mesh: level: 16 (over z_lo, x, core), band: 32 (over y, z_hi).
Axes of the slice: x: 4, y: 8, z: 8 (z_hi: 4, z_lo: 2; z = z_hi * 2 + z_lo), core: 2. Of those that a mesh axis runs over, the one named last changes fastest.
Arguments:
- features: bfloat16 [65536, 128], P('band'), may hold values from -6 to 6
- block_perm: int32 [16, 32, 8], P('level', 'band'), may hold values from 0 to 7, each once within a row
- tile_rows: int32 [16, 1152], P('level', 'band'), may hold values from 0 to 255, as said below
- tile_cols: int32 [16, 1152], P('level', 'band'), may hold values from 0 to 255, as said below
- tile_vals: bfloat16 [16, 1152, 256, 256], P('level', 'band'), may hold values from -0.1875 to 0.1875
Outputs:
- forward: bfloat16 [32, 2048, 128], P('band', 'level')
- backward: bfloat16 [32, 2048, 128], P('band', 'level')
Inputs may be any that keep to these rules, and one draw needn't show every extreme that they name: `block_perm`: each band device's 8 entries of a level are a permutation of 0 to 7. `tile_rows`: the 36 tiles stored at band index b of a level each have either block row in b's blocks [b * 8, (b + 1) * 8) and block column in the blocks of band indices b - 1, b, b + 1 or below 2, or block row below 2 and block column in b's blocks; positions may repeat. `tile_cols`: as for tile_rows, paired entry by entry.
All inputs are finite; a program needn't handle non-finite values.
Results may differ from a plain program's by a relative error of at most 0.001.
Values may be sent and summed in bfloat16 or wider, within the bound.
A program may use at most 128 MiB of HBM per device.

v0:
```python
import jax
import jax.numpy as jnp
from jax import lax
from jax.sharding import PartitionSpec as P

HEADB = 2


def with_halo(block, sides, width):
    for axis, dim in sides:
        count = lax.axis_size(axis)
        forward = [(i, i + 1) for i in range(count - 1)]
        backward = [(target, source) for source, target in forward]
        low = lax.ppermute(
            lax.slice_in_dim(block, block.shape[dim] - width, None, axis=dim), axis, forward
        )
        high = lax.ppermute(lax.slice_in_dim(block, 0, width, axis=dim), axis, backward)
        block = jnp.concatenate([low, block, high], axis=dim)
    return block


def from_root(array, axis, root):
    return lax.dynamic_index_in_dim(lax.all_gather(array, axis), root, 0, keepdims=False)


def passed_along(array, axis, by):
    devices = lax.axis_size(axis)
    pairs = [(i, i + by) for i in range(devices) if 0 <= i + by < devices]
    return lax.ppermute(array, axis, pairs)


def in_blocks(array, dim, devices):
    before, after = (array.shape[:dim], array.shape[dim + 1 :])
    return jnp.moveaxis(array.reshape(*before, devices, -1, *after), dim, 0)


def summed_on_arrival(array, axis, dim):
    parts = in_blocks(array, dim, lax.axis_size(axis))
    arrived = lax.all_to_all(parts, axis, split_axis=0, concat_axis=0, tiled=True)
    return arrived.sum(axis=0)


def rows_for(lines, devices):
    spare = -len(lines) % devices
    return jnp.pad(lines, [(0, spare)] + [(0, 0)] * (lines.ndim - 1))


def from_everyone(array, axis):
    devices = lax.axis_size(axis)
    return lax.all_to_all(
        jnp.broadcast_to(array[None], (devices, *array.shape)), axis, 0, 0, tiled=True
    )


def laid_out(parts, dim):
    parts = jnp.moveaxis(parts, 0, dim)
    shape = parts.shape
    return parts.reshape(*shape[:dim], shape[dim] * shape[dim + 1], *shape[dim + 2 :])


def gather_directly(array, axis, dim):
    parts = from_everyone(array, axis)
    return laid_out(parts, dim)


def sum_by_parts(array, axes):
    own = summed_on_arrival(rows_for(array, lax.axis_size(axes)), axes, 0)
    whole = gather_directly(own, axes, 0)
    return whole[: len(array)].reshape(array.shape)


def packed_total(arrays, axis):
    ends = [0]
    for a in arrays:
        ends.append(ends[-1] + a.size)
    so_far = sum_by_parts(jnp.concatenate([a.ravel() for a in arrays]), axis)
    return tuple((so_far[b:e].reshape(a.shape) for a, b, e in zip(arrays, ends, ends[1:])))


def in_one_piece(arrays, axis, dim, along):
    both = jnp.concatenate(arrays, axis=along)
    whole, at, gathered = (lax.psum_scatter(both, axis, scatter_dimension=dim, tiled=True), 0, [])
    for a in arrays:
        gathered.append(lax.slice_in_dim(whole, at, at + a.shape[along], axis=along))
        at += a.shape[along]
    return tuple(gathered)


def on_device(features, block_perm, tile_rows, tile_cols, tile_vals):
    rdev, width = features.shape
    blocks = block_perm.shape[2]
    tile = tile_vals.shape[2]
    count = tile_vals.shape[1]
    heads = HEADB
    window_len = 3 * blocks + heads
    band_id = lax.axis_index("band")
    perm_local = block_perm[0, 0]
    block_ids = jnp.arange(blocks, dtype=jnp.int32)
    perm_hot = perm_local[:, None] == block_ids[None, :]
    inverse = jnp.sum(jnp.where(perm_hot, block_ids[:, None], 0), axis=0)
    x_blocks = features.reshape(blocks, tile, width)
    level_x = jnp.take(x_blocks, perm_local, axis=0)
    rimmed = with_halo(level_x, (("band", 0),), blocks)
    head_x = from_root(level_x[:heads], "band", 0)
    window = jnp.concatenate([rimmed, head_x], axis=0).reshape(window_len, tile * width)
    rows = tile_rows[0]
    cols = tile_cols[0]
    low = (band_id - 1) * blocks
    near = (cols >= low) & (cols < low + 3 * blocks)
    col_slot = jnp.where(near, cols - low, 3 * blocks + cols)
    own = (rows >= band_id * blocks) & (rows < (band_id + 1) * blocks)
    row_slot = jnp.where(own, rows - low, 3 * blocks + rows)
    by_col = jnp.take(window, col_slot, axis=0).reshape(count, tile, width)
    by_row = jnp.take(window, row_slot, axis=0).reshape(count, tile, width)
    vals = tile_vals[0]
    prod_fwd = jnp.einsum("kij,kjf->kif", vals, by_col, preferred_element_type=jnp.float32)
    prod_bwd = jnp.einsum("kij,kif->kjf", vals, by_row, preferred_element_type=jnp.float32)
    fwd_slot = jnp.where(own, rows - band_id * blocks, blocks + rows)
    fwd_sums = jax.ops.segment_sum(prod_fwd, fwd_slot, num_segments=blocks + heads)
    fwd_local = fwd_sums[:blocks]
    fwd_head = fwd_sums[blocks:]
    bwd_window = jax.ops.segment_sum(prod_bwd, col_slot, num_segments=window_len)
    from_left = passed_along(bwd_window[2 * blocks : 3 * blocks], "band", 1)
    from_right = passed_along(bwd_window[0:blocks], "band", -1)
    bwd_local = bwd_window[blocks : 2 * blocks] + from_left + from_right
    head_fwd, head_bwd = packed_total((fwd_head, bwd_window[3 * blocks :]), "band")
    is_root = (band_id == 0).astype(jnp.float32)
    pad_rows = jnp.zeros((blocks - heads, tile, width), jnp.float32)
    fwd_local = fwd_local + is_root * jnp.concatenate([head_fwd, pad_rows], axis=0)
    bwd_local = bwd_local + is_root * jnp.concatenate([head_bwd, pad_rows], axis=0)
    fwd_global = jnp.take(fwd_local, inverse, axis=0).reshape(rdev, width)
    bwd_global = jnp.take(bwd_local, inverse, axis=0).reshape(rdev, width)
    share = rdev // lax.axis_size("level")
    fwd_mine, bwd_mine = in_one_piece((fwd_global, bwd_global), "level", 0, 1)
    forward = fwd_mine.reshape(1, share, width).astype(jnp.bfloat16)
    backward = bwd_mine.reshape(1, share, width).astype(jnp.bfloat16)
    return (forward, backward)


def solution(mesh):
    return jax.shard_map(
        on_device,
        mesh=mesh,
        in_specs=(
            P("band", None),
            P("level", "band", None),
            P("level", "band"),
            P("level", "band"),
            P("level", "band", None, None),
        ),
        out_specs=(P("band", "level", None), P("band", "level", None)),
        check_vma=False,
    )
```

profile of v0, /device:TPU:1, one launch (start us, length us, event | category | flops | bytes accessed | tf_op | source)
XLA Modules:
  0.0 374.4 jit_solution(17547259215249994756)
XLA Ops:
  7.2 0.7 compare_and_fusion.3
  7.9 0.7 fusion.18
  8.6 0.6 gather_fusion
  9.4 0.7 slice.62
  10.1 1.3 collective-permute-start.1
  11.4 7.3 %collective-permute-start = (bf16[8,256,128]{2,1,0:T(8,128)(2,1)S(1)}, bf16[8,256,128]{2,1,0:T(8,128)(2,1)S(1)}, u32[]{:S(2)}, u32[]{:S(2)}) collective-permute-start(bf16[8,256,128]{2,1,0:T(8,128)(2,1)S(1)} %broadcast_select_fusion.4), channel_id=1, source_target_pairs={{0,1},{1,2},{2,3},{3,4},{4,5},{5,6},{6,7},{7,8},{8,9},{9,10},{10,1... | collective-permute-start | bytes 1572872 | tf_op jit(solution)/shard_map/ppermute | solution.py:14
  18.7 0.7 compare_and_fusion.1
  19.4 1.1 bitcast_select_fusion
  20.6 21.0 %collective-permute-done.1 = bf16[8,256,128]{2,1,0:T(8,128)(2,1)S(1)} collective-permute-done((bf16[8,256,128]{2,1,0:T(8,128)(2,1)S(1)}, bf16[8,256,128]{2,1,0:T(8,128)(2,1)S(1)}, u32[]{:S(2)}, u32[]{:S(2)}) %collective-permute-start.1) | collective-permute-done | bytes 524320 | tf_op jit(solution)/shard_map/ppermute | solution.py:17
  41.5 0.3 copy.31
  41.9 0.3 copy.32
  42.2 90.8 %all-gather.3.cloned.1.call-done = bf16[64,256,128]{2,1,0:T(8,128)(2,1)} async-done(((bf16[2,256,128]{2,1,0:T(8,128)(2,1)}), bf16[64,256,128]{2,1,0:T(8,128)(2,1)}) %all-gather.3.cloned.1.call-update) | async-done | bytes 4194320 | tf_op jit(solution)/shard_map/all_gather | solution.py:23
  133.1 0.9 slice_bitcast_fusion
  134.0 0.1 copy.33
  134.1 1.2 pad_maximum_fusion
  135.4 3.6 gather_fusion.2
  139.0 2.1 broadcast_select_fusion
  141.1 2.1 copy.26
  143.2 3.6 gather_fusion.1
  146.8 2.0 broadcast_select_fusion.1
  148.9 0.6 copy.25
  149.5 6.2 %fusion.6 = f32[36,256,128]{1,2,0:T(8,128)} fusion(bf16[1,36,256,256]{3,2,1,0:T(8,128)(2,1)} %param.13, bf16[40,256,128]{2,1,0:T(8,128)(2,1)S(1)} %bitcast.62), kind=kOutput, calls=%fused_computation.15 | convolution fusion | flops 603979776 | bytes 11796480 | tf_op jit(solution)/shard_map/kij,kjf->kif/dot_general | solution.py:116
  155.7 6.1 %copy.16 = f32[36,256,128]{2,1,0:T(8,128)} copy(f32[36,256,128]{1,2,0:T(8,128)} %fusion.6) | data formatting | bytes 9437184 | tf_op jit(solution)/shard_map/kij,kjf->kif/dot_general | solution.py:116
  161.9 8.8 %scatter_fusion = f32[10,256,128]{2,1,0:T(8,128)S(1)} fusion(f32[10,256,128]{2,1,0:T(8,128)S(1)} %broadcast_in_dim.61, s32[36]{0:T(128)S(1)} %select_bitcast_fusion, f32[36,256,128]{2,1,0:T(8,128)} %copy.16), kind=kCustom, calls=%fused_computation.5 | custom fusion | flops 1179648 | bytes 14155920 | tf_op jit(solution)/shard_map/scatter-add | solution.py:119
  170.9 6.2 %fusion.11 = f32[36,256,128]{1,2,0:T(8,128)} fusion(bf16[1,36,256,256]{3,2,1,0:T(8,128)(2,1)} %param.13, bf16[40,256,128]{2,1,0:T(8,128)(2,1)} %bitcast.61), kind=kOutput, calls=%fused_computation.16 | convolution fusion | flops 603979776 | bytes 11796480 | tf_op jit(solution)/shard_map/kij,kif->kjf/dot_general | solution.py:117
  177.0 6.0 %copy.18 = f32[36,256,128]{2,1,0:T(8,128)} copy(f32[36,256,128]{1,2,0:T(8,128)} %fusion.11) | data formatting | bytes 9437184 | tf_op jit(solution)/shard_map/kij,kif->kjf/dot_general | solution.py:117
  183.1 2.1 broadcast_in_dim.66
  185.2 14.4 %scatter_fusion.1 = f32[26,256,128]{2,1,0:T(8,128)} fusion(f32[26,256,128]{2,1,0:T(8,128)} %broadcast_in_dim.66, s32[36]{0:T(128)S(1)} %get-tuple-element.17, f32[36,256,128]{2,1,0:T(8,128)} %copy.18), kind=kCustom, calls=%fused_computation.6 | custom fusion | flops 1179648 | bytes 14155920 | tf_op jit(solution)/shard_map/scatter-add | solution.py:122
  199.6 1.0 slice.66
  200.7 0.6 all_to_all.10
  201.3 21.8 %all_to_all.15 = f32[32,1,4096]{2,1,0:T(1,128)S(1)} all-to-all(f32[32,1,4096]{2,1,0:T(1,128)S(1)} %all_to_all.10), channel_id=1, replica_groups=mesh['level'=16,'band'=32] {'band'}, dimensions={0} | all-to-all | bytes 1048576 | tf_op jit(solution)/shard_map/all_to_all | solution.py:39
  223.0 0.4 reduce_sum.18
  223.4 1.3 broadcast_in_dim.67
  224.7 7.2 %all-to-all-start.1 = ((f32[32,1,4096]{2,1,0:T(1,128)}), f32[32,1,4096]{2,1,0:T(1,128)S(1)}, u32[]{:S(2)}, u32[]{:S(2)}) async-start(f32[32,1,4096]{2,1,0:T(1,128)} %broadcast_in_dim.67), calls=%async_computation.1 | async-start | bytes 1048576 | tf_op jit(solution)/shard_map/all_to_all | solution.py:50
  232.1 3.1 fusion.21
  235.2 5.1 %collective-permute-start.2 = (f32[8,256,128]{2,1,0:T(8,128)}, f32[8,256,128]{2,1,0:T(8,128)}, u32[]{:S(2)}, u32[]{:S(2)}) collective-permute-start(f32[8,256,128]{2,1,0:T(8,128)} %get-tuple-element.8), channel_id=1, source_target_pairs={{0,1},{1,2},{2,3},{3,4},{4,5},{5,6},{6,7},{7,8},{8,9},{9,10},{10,1... | collective-permute-start | bytes 3145736 | tf_op jit(solution)/shard_map/ppermute | solution.py:29
  240.2 1.3 collective-permute-start.3
  241.5 6.3 %all-to-all-done.1 = f32[32,1,4096]{2,1,0:T(1,128)S(1)} async-done(((f32[32,1,4096]{2,1,0:T(1,128)}), f32[32,1,4096]{2,1,0:T(1,128)S(1)}, u32[]{:S(2)}, u32[]{:S(2)}) %all-to-all-start.1) | async-done | bytes 524320 | tf_op jit(solution)/shard_map/all_to_all | solution.py:50
  247.9 0.6 gather_fusion.3
  248.5 21.1 %collective-permute-done.2 = f32[8,256,128]{2,1,0:T(8,128)} collective-permute-done((f32[8,256,128]{2,1,0:T(8,128)}, f32[8,256,128]{2,1,0:T(8,128)}, u32[]{:S(2)}, u32[]{:S(2)}) %collective-permute-start.2) | collective-permute-done | bytes 1048608 | tf_op jit(solution)/shard_map/ppermute | solution.py:29
  269.6 25.1 %collective-permute-done.3 = f32[8,256,128]{2,1,0:T(8,128)} collective-permute-done((f32[8,256,128]{2,1,0:T(8,128)}, f32[8,256,128]{2,1,0:T(8,128)}, u32[]{:S(2)}, u32[]{:S(2)}) %collective-permute-start.3) | collective-permute-done | bytes 1048608 | tf_op jit(solution)/shard_map/ppermute | solution.py:29
  294.7 2.0 fusion.17
  296.7 1.6 gather_fusion.4
  298.3 1.5 broadcast_select_fusion.3
  299.8 1.5 pad_maximum_fusion.1
  301.3 64.7 %reduce-scatter.2.cloned.1.call-done = f32[128,256]{1,0:T(8,128)} async-done(((f32[2048,256]{1,0:T(8,128)}), f32[128,256]{1,0:T(8,128)}) %reduce-scatter.2.cloned.1.call-update) | async-done | bytes 131088 | tf_op jit(solution)/shard_map/reduce_scatter | solution.py:82
  366.0 0.9 convert.4
  366.9 0.6 slice_bitcast_fusion.1
  (30 shorter events, 0.8 us)
Async XLA Ops:
  7.2 1.5 copy-start
  7.2 13.3 %copy-start.2 = (s32[1,36]{1,0:T(1,128)S(1)}, s32[1,36]{1,0:T(1,128)}, u32[]{:S(2)}) copy-start(s32[1,36]{1,0:T(1,128)} %param.11) | copy-start | bytes 436
  7.2 125.9 %all-gather.3.cloned.1.call-start = ((), (), s32[]{:S(2)}) async-start(), calls=%async_computation.4 | async-start | bytes 4325376 | tf_op jit(solution)/shard_map/all_gather | solution.py:23
  10.1 31.4 %collective-permute-start.1 = (bf16[8,256,128]{2,1,0:T(8,128)(2,1)S(1)}, bf16[8,256,128]{2,1,0:T(8,128)(2,1)S(1)}, u32[]{:S(2)}, u32[]{:S(2)}) collective-permute-start(bf16[8,256,128]{2,1,0:T(8,128)(2,1)S(1)} %broadcast_select_fusion.4), channel_id=1, source_target_pairs={{1,0},{2,1},{3,2},{4,3},{5,4},{6,5},{7,6},{8,7},{9,8},{10,9},{11,1... | collective-permute-start | bytes 1572872 | tf_op jit(solution)/shard_map/ppermute | solution.py:17
  11.4 30.5 %collective-permute-start = (bf16[8,256,128]{2,1,0:T(8,128)(2,1)S(1)}, bf16[8,256,128]{2,1,0:T(8,128)(2,1)S(1)}, u32[]{:S(2)}, u32[]{:S(2)}) collective-permute-start(bf16[8,256,128]{2,1,0:T(8,128)(2,1)S(1)} %broadcast_select_fusion.4), channel_id=1, source_target_pairs={{0,1},{1,2},{2,3},{3,4},{4,5},{5,6},{6,7},{7,8},{8,9},{9,10},{10,1... | collective-permute-start | bytes 1572872 | tf_op jit(solution)/shard_map/ppermute | solution.py:14
  200.7 31.3 %copy-start.3 = (s32[1,1,8]{2,1,0:T(1,128)S(1)}, s32[1,1,8]{2,1,0:T(1,128)}, u32[]{:S(2)}) copy-start(s32[1,1,8]{2,1,0:T(1,128)} %param.10) | copy-start | bytes 100
  224.7 23.1 %all-to-all-start.1 = ((f32[32,1,4096]{2,1,0:T(1,128)}), f32[32,1,4096]{2,1,0:T(1,128)S(1)}, u32[]{:S(2)}, u32[]{:S(2)}) async-start(f32[32,1,4096]{2,1,0:T(1,128)} %broadcast_in_dim.67), calls=%async_computation.1 | async-start | bytes 1048576 | tf_op jit(solution)/shard_map/all_to_all | solution.py:50
  231.9 134.1 %reduce-scatter.2.cloned.1.call-start = ((), (), s32[]{:S(2)}) async-start(), calls=%async_computation.3 | async-start | bytes 2228224 | tf_op jit(solution)/shard_map/reduce_scatter | solution.py:82
  235.2 34.5 %collective-permute-start.2 = (f32[8,256,128]{2,1,0:T(8,128)}, f32[8,256,128]{2,1,0:T(8,128)}, u32[]{:S(2)}, u32[]{:S(2)}) collective-permute-start(f32[8,256,128]{2,1,0:T(8,128)} %get-tuple-element.8), channel_id=1, source_target_pairs={{0,1},{1,2},{2,3},{3,4},{4,5},{5,6},{6,7},{7,8},{8,9},{9,10},{10,1... | collective-permute-start | bytes 3145736 | tf_op jit(solution)/shard_map/ppermute | solution.py:29
  240.2 54.5 %collective-permute-start.3 = (f32[8,256,128]{2,1,0:T(8,128)}, f32[8,256,128]{2,1,0:T(8,128)}, u32[]{:S(2)}, u32[]{:S(2)}) collective-permute-start(f32[8,256,128]{2,1,0:T(8,128)} %get-tuple-element.9), channel_id=1, source_target_pairs={{1,0},{2,1},{3,2},{4,3},{5,4},{6,5},{7,6},{8,7},{9,8},{10,9},{11,1... | collective-permute-start | bytes 3145736 | tf_op jit(solution)/shard_map/ppermute | solution.py:29
  299.8 67.8 %copy-start.1 = (bf16[2048,128]{1,0:T(8,128)(2,1)S(1)}, bf16[2048,128]{1,0:T(8,128)(2,1)}, u32[]{:S(2)}) copy-start(bf16[2048,128]{1,0:T(8,128)(2,1)} %param.9) | copy-start | bytes 1572868
Sparse Core Ops, SparseCore 0:
  11.2 121.8 all-gather.2
  301.4 64.5 reduce-scatter.1
where the time goes:
time: 377 us; the launch traced here: 374 us
  waiting for transfers between devices  229 us (61%)
  other arithmetic  38.4 us (10%)
  local copies, waits for them, and re-layouts  36.3 us (10%)
  starting transfers between devices  22.3 us (6%)
  blocking collectives  21.8 us (6%)
  between operations  14.3 us (4%)
  matrix products  12.4 us (3%)
    all_gather x1, waiting for transfers between devices, from_root(): lax.all_gather(array, axis)  90.8 us
    reduce_scatter x1, waiting for transfers between devices, in_one_piece(): lax.psum_scatter(both, axis, scatter_dimension=dim, tiled=True)  64.7 us
    ppermute x2, waiting for transfers between devices, passed_along(): return lax.ppermute(array, axis, pairs)  46.2 us
    all_to_all x1, blocking collectives, summed_on_arrival(): lax.all_to_all(parts, axis, split_axis=0, concat_axis=0, tiled=True)  21.8 us
    ppermute x1, waiting for transfers between devices, with_halo(): lax.ppermute(lax.slice_in_dim(block, 0, width, axis=dim), axis, backward)  21 us
    scatter-add x1, other arithmetic, on_device(): jax.ops.segment_sum(prod_bwd, col_slot, num_segments=window_len)  14.4 us
    scatter-add x1, other arithmetic, on_device(): jax.ops.segment_sum(prod_fwd, fwd_slot, num_segments=blocks + heads)  8.83 us
  transfers between devices with their start and end apart: 7, of which 6 were waited for; matrix products, arithmetic and copies ran while one was open for 2% of the time, Pallas kernels for 0%

commit v1 on v0

v1 whole, which is shorter than its diff:
```python
import jax
import jax.numpy as jnp
from jax import lax
from jax.experimental import pallas as pl
from jax.experimental.pallas import tpu as pltpu
from jax.sharding import PartitionSpec as P

MESH = pl.DeviceIdType.MESH
NX, NY, NZ = 4, 8, 4
LEVELS, BANDS = 16, 32
RB, HALF, F, TILE, K = 8, 128, 128, 256, 36
UNITS = 6
Z_FIRST = (True, False, True, False, True, False)


def place():
    level = lax.axis_index("level")
    band = lax.axis_index("band")
    return level, band, level // 8, (level // 2) % NX, level % 2, band // NZ, band % NZ


def dev(level, band):
    return {"level": level, "band": band}


def remote(src, dst, send, recv, to):
    return pltpu.make_async_remote_copy(
        src_ref=src, dst_ref=dst, send_sem=send, recv_sem=recv, device_id=to, device_id_type=MESH
    )


def greet(barrier, to):
    pl.semaphore_signal(barrier, inc=1, device_id=to, device_id_type=MESH)


def at_x(level, x):
    return (level // 8) * 8 + x * 2 + level % 2


def gather_kernel(feat, perm, xs, perms, own_sem, near_s, near_r, core_s, core_r, far_s, far_r,
                  p_s, p_r, h1_s, h1_r, h2_s, h2_r, q1_s, q1_r, q2_s, q2_r, hz_s, hz_r, hx_s, hx_r,
                  hc_s, hc_r):
    level, band, zl, x, c, y, zh = place()
    flip = lax.rem(level + 8, LEVELS)
    near_band = lax.rem(band + jnp.where(zl == 0, BANDS - 1, 1), BANDS)
    up = lax.rem(band + 1, BANDS)
    down = lax.rem(band + BANDS - 1, BANDS)
    near_dev = dev(flip, near_band)
    pair_dev = dev(flip, band)
    core_dev = dev(level + 1 - 2 * c, band)
    x_devs = [dev(at_x(level, lax.rem(x + d, NX)), band) for d in (1, 2, 3)]
    barrier = pltpu.get_barrier_semaphore()
    for to in (near_dev, pair_dev, core_dev, *x_devs, dev(level, up), dev(level, down)):
        greet(barrier, to)

    @pl.when(band == 0)
    def _():
        for d in range(1, NZ):
            greet(barrier, dev(level, d))

    @pl.when((y == 0) & (zh != 0))
    def _():
        greet(barrier, dev(level, 0))

    @pl.when(y == 0)
    def _():
        for d in range(1, NY):
            greet(barrier, dev(level, d * NZ + zh))

    @pl.when(y != 0)
    def _():
        greet(barrier, dev(level, zh))

    pl.semaphore_wait(
        barrier, 8 + jnp.where(y == 0, jnp.where(zh == 0, NZ - 1 + NY - 1, 1 + NY - 1), 1)
    )

    own = pltpu.make_async_copy(feat, xs.at[1], own_sem.at[0])
    own.start()
    own_p = pltpu.make_async_copy(perm, perms.at[1], own_sem.at[1])
    own_p.start()
    to_up = remote(perm, perms.at[0], p_s.at[0], p_r.at[0], dev(level, up))
    to_down = remote(perm, perms.at[2], p_s.at[1], p_r.at[1], dev(level, down))
    to_up.start()
    to_down.start()
    near = [
        remote(feat.at[c, i], xs.at[0, c, i], near_s.at[i], near_r.at[i], near_dev)
        for i in range(NX)
    ]

    @pl.when(band == 0)
    def _():
        piece = pltpu.make_async_copy(feat.at[zl, x, c], xs.at[3, zl, x, c], own_sem.at[2])
        piece.start()
        first = pltpu.make_async_copy(perm, perms.at[3], own_sem.at[3])
        first.start()
        for d in range(1, NZ):
            remote(feat.at[zl, x, c], xs.at[3, zl, x, c], h1_s.at[d - 1], h1_r.at[0], dev(level, d)).start()
            remote(perm, perms.at[3], q1_s.at[d - 1], q1_r.at[0], dev(level, d)).start()
        piece.wait()
        first.wait()

    for copy in near:
        copy.start()
    h1_in = remote(feat.at[zl, x, c], xs.at[3, zl, x, c], h1_s.at[0], h1_r.at[0], dev(level, 0))
    q1_in = remote(perm, perms.at[3], q1_s.at[0], q1_r.at[0], dev(level, 0))

    @pl.when((y == 0) & (zh != 0))
    def _():
        h1_in.wait_recv()
        q1_in.wait_recv()

    def fan(d):
        to = dev(level, d * NZ + zh)
        return (
            remote(xs.at[3, zl, x, c], xs.at[3, zl, x, c], h2_s.at[d - 1], h2_r.at[0], to),
            remote(perms.at[3], perms.at[3], q2_s.at[d - 1], q2_r.at[0], to),
        )

    @pl.when(y == 0)
    def _():
        for d in range(1, NY):
            for copy in fan(d):
                copy.start()

    far = [
        remote(xs.at[0, c, i], xs.at[2, c, i], far_s.at[i], far_r.at[i], pair_dev) for i in range(NX)
    ]
    core = [
        remote(xs.at[s, c, i], xs.at[s, c, i], core_s.at[j, i], core_r.at[j, i], core_dev)
        for j, s in enumerate((0, 2))
        for i in range(NX)
    ]
    core_in = [
        remote(xs.at[s, 1 - c, i], xs.at[s, 1 - c, i], core_s.at[j, i], core_r.at[j, i], core_dev)
        for j, s in enumerate((0, 2))
        for i in range(NX)
    ]
    for i in range(NX):
        near[i].wait_recv()
        far[i].start()
        core[i].start()

    @pl.when(y != 0)
    def _():
        for copy in fan(1):
            copy.wait_recv()

    h_pair = remote(xs.at[3, zl, x, c], xs.at[3, zl, x, c], hz_s, hz_r, pair_dev)
    h_pair.start()
    for i in range(NX):
        far[i].wait_recv()
        core[NX + i].start()
    remote(xs.at[3, 1 - zl, x, c], xs.at[3, 1 - zl, x, c], hz_s, hz_r, pair_dev).wait_recv()
    h_x = []
    for d in range(3):
        copy = remote(xs.at[3, :, x, c], xs.at[3, :, x, c], hx_s.at[d], hx_r.at[d], x_devs[d])
        copy.start()
        h_x.append(copy)
    for d in range(3):
        source = lax.rem(x + NX - 1 - d, NX)
        remote(xs.at[3, :, source, c], xs.at[3, :, source, c], hx_s.at[d], hx_r.at[d], x_devs[d]).wait_recv()
    h_core = remote(xs.at[3, :, :, c], xs.at[3, :, :, c], hc_s, hc_r, core_dev)
    h_core.start()
    own.wait()
    own_p.wait()
    to_up.wait()
    to_down.wait()
    for copy in core_in:
        copy.wait_recv()
    remote(xs.at[3, :, :, 1 - c], xs.at[3, :, :, 1 - c], hc_s, hc_r, core_dev).wait_recv()
    for copy in (*near, *far, *core, h_pair, *h_x, h_core):
        copy.wait_send()

    @pl.when(band == 0)
    def _():
        for d in range(1, NZ):
            remote(feat.at[zl, x, c], xs.at[3, zl, x, c], h1_s.at[d - 1], h1_r.at[0], dev(level, d)).wait_send()
            remote(perm, perms.at[3], q1_s.at[d - 1], q1_r.at[0], dev(level, d)).wait_send()

    @pl.when(y == 0)
    def _():
        for d in range(1, NY):
            for copy in fan(d):
                copy.wait_send()


def product_kernel(rows, cols, perms, xs, vals, sums, held, sems):
    level, band, zl, x, c, y, zh = place()
    groups = 6
    each = K // groups
    loads = [
        pltpu.make_async_copy(vals.at[pl.ds(g * each, each)], held.at[pl.ds(g * each, each)], sems.at[g])
        for g in range(groups)
    ]
    for load in loads:
        load.start()
    sums[...] = jnp.zeros_like(sums)
    low = (band - 1) * RB

    def tile_step(k, carry):
        row, col = rows[0, k], cols[0, k]
        own = (row >= band * RB) & (row < (band + 1) * RB)
        near = (col >= low) & (col < low + 3 * RB)
        r_slot = jnp.where(own, 1, 3)
        r_block = perms[r_slot, 0, jnp.where(own, row - band * RB, row)]
        rel = col - low
        side = jnp.where(near, rel // RB, 3)
        c_block = perms[side, 0, jnp.where(near, rel % RB, col)]
        x_slot = jnp.where(side == 1, 1, jnp.where(side == 3, 3, jnp.where((side == 0) == (zl == 0), 0, 2)))
        a = held[k]
        fwd = jnp.dot(a, xs[x_slot * RB + c_block], preferred_element_type=jnp.float32)
        f_out = jnp.where(own, 4, 0) * RB + r_block
        sums[f_out] += fwd
        bwd = lax.dot_general(
            a, xs[r_slot * RB + r_block], (((0,), (0,)), ((), ())), preferred_element_type=jnp.float32
        )
        b_win = jnp.where(side == 1, 5, jnp.where(side == 0, 2, jnp.where(side == 2, 3, 1)))
        b_out = b_win * RB + c_block
        sums[b_out] += bwd
        return carry

    for g in range(groups):
        loads[g].wait()
        lax.fori_loop(g * each, (g + 1) * each, tile_step, 0)


def reduce_kernel(w, fwd_out, bwd_out, rc, rz, xa, xb, acc, tot, ry, hs, rzh, rr, rl, rrt,
                  c_s, c_r, z_s, z_r, a_s, a_r, b_s, b_r, s_s, s_r, y_s, y_r, q_s, q_r, t_s, t_r):
    level, band, zl, x, c, y, zh = place()
    flip = lax.rem(level + 8, LEVELS)
    up = dev(level, lax.rem(band + 1, BANDS))
    down = dev(level, lax.rem(band + BANDS - 1, BANDS))
    pair_dev = dev(flip, band)
    core_dev = dev(level + 1 - 2 * c, band)
    xp, xm, xf = lax.rem(x + 1, NX), lax.rem(x + 3, NX), lax.rem(x + 2, NX)
    x_up, x_down = dev(at_x(level, xp), band), dev(at_x(level, xm), band)
    y_devs = [dev(level, lax.rem(y + d, NY) * NZ + zh) for d in range(1, NY)]
    barrier = pltpu.get_barrier_semaphore()
    for to in (pair_dev, core_dev, x_up, x_down, up, down, *y_devs):
        greet(barrier, to)

    @pl.when(zh == 0)
    def _():
        for d in range(1, NZ):
            greet(barrier, dev(level, band + d))

    @pl.when(zh != 0)
    def _():
        greet(barrier, dev(level, y * NZ))

    pl.semaphore_wait(barrier, 6 + NY - 1 + jnp.where(zh == 0, NZ - 1, 1))

    sent = []

    def send(*args):
        copy = remote(*args)
        copy.start()
        sent.append(copy)
        return copy

    core = [
        send(w.at[u, :, :, 1 - c], rc.at[u], c_s.at[u], c_r.at[u], core_dev) for u in range(UNITS)
    ]
    pending = {}

    def ring_start(u, piece, n):
        half = HALF // 2
        pending[u] = [
            send(piece(xf).at[:, pl.ds(0, half)], xa.at[u, 0, pl.ds(0, n)], a_s.at[u, 0], a_r.at[u, 0], x_up),
            send(piece(xf).at[:, pl.ds(half, half)], xa.at[u, 1, pl.ds(0, n)], a_s.at[u, 1], a_r.at[u, 1], x_down),
        ]

    def ring_pass(u, piece, n):
        half = HALF // 2
        for copy in pending[u]:
            copy.wait_recv()
        low = piece(xp).at[:, pl.ds(0, half)]
        low[...] += xa[u, 0, :n]
        high = piece(xm).at[:, pl.ds(half, half)]
        high[...] += xa[u, 1, :n]
        pending[u] = [
            send(piece(xp), xb.at[u, 0, pl.ds(0, n)], b_s.at[u, 0], b_r.at[u, 0], x_up),
            send(piece(xm), xb.at[u, 1, pl.ds(0, n)], b_s.at[u, 1], b_r.at[u, 1], x_down),
        ]

    def ring_end(u, piece, n):
        for copy in pending[u]:
            copy.wait_recv()
        return piece(x)[...] + xb[u, 0, :n] + xb[u, 1, :n]

    def z_piece(u):
        return lambda i: acc.at[u, pl.ds(i, 1)]

    def x_piece(u):
        return lambda i: rc.at[u, :, i]

    def step0(u):
        core[u].wait_recv()
        rc[u] += w[u, :, :, c]
        if Z_FIRST[u]:
            pending[u] = [send(rc.at[u, 1 - zl], rz.at[u], z_s.at[u], z_r.at[u], pair_dev)]
        else:
            ring_start(u, x_piece(u), 2)

    def step1(u):
        if Z_FIRST[u]:
            pending[u][0].wait_recv()
            acc[u] = rc[u, zl] + rz[u]
            ring_start(u, z_piece(u), 1)
        else:
            ring_pass(u, x_piece(u), 2)

    def step2(u):
        if Z_FIRST[u]:
            ring_pass(u, z_piece(u), 1)
        else:
            acc[u, pl.ds(0, 2)] = ring_end(u, x_piece(u), 2)
            pending[u] = [
                send(acc.at[u, pl.ds(1 - zl, 1)], rz.at[u, pl.ds(0, 1)], z_s.at[u], z_r.at[u], pair_dev)
            ]

    def step3(u):
        if Z_FIRST[u]:
            tot[u] = ring_end(u, z_piece(u), 1)[0].reshape(NY, HALF // NY, F)
        else:
            pending[u][0].wait_recv()
            tot[u] = (acc[u, zl] + rz[u, 0]).reshape(NY, HALF // NY, F)

    for u in range(UNITS):
        step0(u)
    for u in (0, 1):
        step1(u)
    for u in (0, 1):
        step2(u)
    for u in (2, 3):
        step1(u)
    for u in (0, 1):
        step3(u)
    y_in = []
    for d in range(1, NY):
        y_in.append(
            send(tot.at[pl.ds(0, 2), lax.rem(y + d, NY)], ry.at[d - 1], y_s.at[d - 1], y_r.at[d - 1], y_devs[d - 1])
        )
    for u in (2, 3):
        step2(u)
    for u in (4, 5):
        step1(u)
    for u in (2, 3):
        step3(u)
    side_r = send(tot.at[3], rl, s_s.at[0], s_r.at[0], up)
    side_l = send(tot.at[2], rrt, s_s.at[1], s_r.at[1], down)
    for copy in y_in:
        copy.wait_recv()
    hs[...] = tot[pl.ds(0, 2), y] + jnp.sum(ry[...], axis=0)

    def up_z():
        return remote(hs, rzh.at[zh - 1], q_s, q_r.at[zh - 1], dev(level, y * NZ))

    def to_root():
        return remote(hs, rr.at[y - 1], t_s, t_r.at[y - 1], dev(level, 0))

    @pl.when(zh != 0)
    def _():
        up_z().start()

    for u in (4, 5):
        step2(u)

    @pl.when(zh == 0)
    def _():
        for d in range(NZ - 1):
            remote(hs, rzh.at[d], q_s, q_r.at[d], dev(level, y * NZ + d + 1)).wait_recv()
        hs[...] += jnp.sum(rzh[...], axis=0)

    @pl.when((zh == 0) & (y != 0))
    def _():
        to_root().start()

    for u in (4, 5):
        step3(u)
    side_r.wait_recv()
    side_l.wait_recv()
    tot[5] += rl[...] + rrt[...]

    @pl.when(band == 0)
    def _():
        for d in range(NY - 1):
            remote(hs, rr.at[d], t_s, t_r.at[d], dev(level, (d + 1) * NZ)).wait_recv()
        for j in range(2):
            tot[4 + j, 0] += hs[j]
            for d in range(1, NY):
                tot[4 + j, d] += rr[d - 1, j]

    fwd_out[...] = tot[4].reshape(HALF, F).astype(jnp.bfloat16)
    bwd_out[...] = tot[5].reshape(HALF, F).astype(jnp.bfloat16)
    for copy in sent:
        copy.wait_send()

    @pl.when(zh != 0)
    def _():
        up_z().wait_send()

    @pl.when((zh == 0) & (y != 0))
    def _():
        to_root().wait_send()


def on_device(features, block_perm, tile_rows, tile_cols, tile_vals):
    vmem = pl.BlockSpec(memory_space=pltpu.VMEM)
    smem = pl.BlockSpec(memory_space=pltpu.SMEM)
    dma = pltpu.SemaphoreType.DMA
    perm = jnp.pad(block_perm[0], ((0, 7), (0, 128 - RB)))
    feat = features.reshape(2, NX, 2, HALF, F)
    xs, perms = pl.pallas_call(
        gather_kernel,
        out_shape=(
            jax.ShapeDtypeStruct((4, 2, NX, 2, HALF, F), jnp.bfloat16),
            jax.ShapeDtypeStruct((4, 8, 128), jnp.int32),
        ),
        in_specs=[vmem, vmem],
        out_specs=(vmem, vmem),
        scratch_shapes=[
            dma((4,)), dma((4,)), dma((4,)), dma((2, 4)), dma((2, 4)), dma((4,)), dma((4,)),
            dma((2,)), dma((2,)), dma((3,)), dma((1,)), dma((7,)), dma((1,)), dma((3,)), dma((1,)),
            dma((7,)), dma((1,)), dma(()), dma(()), dma((3,)), dma((3,)), dma(()), dma(()),
        ],
        compiler_params=pltpu.CompilerParams(collective_id=0, has_side_effects=True),
        name="gather",
    )(feat, perm)
    sums = pl.pallas_call(
        product_kernel,
        out_shape=jax.ShapeDtypeStruct((UNITS * RB, TILE, F), jnp.float32),
        in_specs=[smem, smem, smem, vmem, pl.BlockSpec(memory_space=pl.ANY)],
        out_specs=vmem,
        scratch_shapes=[pltpu.VMEM((K, TILE, TILE), jnp.bfloat16), dma((6,))],
        name="products",
    )(tile_rows, tile_cols, perms, xs.reshape(4 * RB, TILE, F), tile_vals[0])
    f32 = jnp.float32
    part = HALF // NY
    fwd, bwd = pl.pallas_call(
        reduce_kernel,
        out_shape=(jax.ShapeDtypeStruct((HALF, F), jnp.bfloat16),) * 2,
        in_specs=[vmem],
        out_specs=(vmem, vmem),
        scratch_shapes=[
            pltpu.VMEM((UNITS, 2, NX, HALF, F), f32),
            pltpu.VMEM((UNITS, NX, HALF, F), f32),
            pltpu.VMEM((UNITS, 2, 2, HALF // 2, F), f32),
            pltpu.VMEM((UNITS, 2, 2, HALF, F), f32),
            pltpu.VMEM((UNITS, NX, HALF, F), f32),
            pltpu.VMEM((UNITS, NY, part, F), f32),
            pltpu.VMEM((NY - 1, 2, part, F), f32),
            pltpu.VMEM((2, part, F), f32),
            pltpu.VMEM((NZ - 1, 2, part, F), f32),
            pltpu.VMEM((NY - 1, 2, part, F), f32),
            pltpu.VMEM((NY, part, F), f32),
            pltpu.VMEM((NY, part, F), f32),
            dma((6,)), dma((6,)), dma((6,)), dma((6,)), dma((6, 2)), dma((6, 2)), dma((6, 2)), dma((6, 2)),
            dma((2,)), dma((2,)), dma((7,)), dma((7,)), dma(()), dma((3,)), dma(()), dma((7,)),
        ],
        compiler_params=pltpu.CompilerParams(collective_id=1, has_side_effects=True),
        name="reduce",
    )(sums.reshape(UNITS, 2, NX, 2, HALF, F))
    return fwd[None], bwd[None]


def solution(mesh):
    return jax.shard_map(
        on_device,
        mesh=mesh,
        in_specs=(
            P("band", None),
            P("level", "band", None),
            P("level", "band"),
            P("level", "band"),
            P("level", "band", None, None),
        ),
        out_specs=(P("band", "level", None), P("band", "level", None)),
        check_vma=False,
    )
```

time: 377 us -> 104 us (0.28)
  waiting for transfers between devices: 229 us -> 0 us
  Pallas kernels: 0 us -> 99.2 us
  other arithmetic: 38.4 us -> 0 us
  local copies, waits for them, and re-layouts: 36.3 us -> 4 us
  starting transfers between devices: 22.3 us -> 0 us
  blocking collectives: 21.8 us -> 0 us
  between operations: 14.3 us -> 0.65 us
  matrix products: 12.4 us -> 0 us
    pallas_call x0 -> x3, Pallas kernels: none -> 99.2 us  [the longest x1 50.9 us: on_device(): pl.pallas_call(reduce_kernel, out_shape=(jax.ShapeDtypeStruct((HALF, F),...]
    all_gather x1 -> x0, waiting for transfers between devices: 90.8 us -> none  [from_root(): lax.all_gather(array, axis)]
    ppermute x4 -> x0, waiting for transfers between devices: 67.1 us -> none  [the longest x2 46.2 us: passed_along(): return lax.ppermute(array, axis, pairs)]
    reduce_scatter x1 -> x0, waiting for transfers between devices: 64.7 us -> none  [in_one_piece(): lax.psum_scatter(both, axis, scatter_dimension=dim, tiled=True)]
    scatter-add x2 -> x0, other arithmetic: 23.3 us -> none  [the longest x1 14.4 us: on_device(): jax.ops.segment_sum(prod_bwd, col_slot, num_segments=window_len)]
    all_to_all x1 -> x0, blocking collectives: 21.8 us -> none  [summed_on_arrival(): lax.all_to_all(parts, axis, split_axis=0, concat_axis=0, tiled=True)]
    ppermute x4 -> x0, starting transfers between devices: 14.9 us -> none  [the longest x1 7.28 us: with_halo(): lax.ppermute(lax.slice_in_dim(block, block.shape[dim] - width, None, axis...]
    dot_general x2 -> x0, matrix products: 12.4 us -> none  [the longest x1 6.21 us: on_device(): jnp.einsum('kij,kjf->kif', vals, by_col, preferred_element_type=jnp.float32)]
  transfers between devices with their start and end apart: 7 -> 0, of which waited for: 6 -> 0; matrix products, arithmetic and copies ran while one was open for 2% -> 0% of each run, Pallas kernels for 0% -> 0%
where the time goes in v1:
time: 104 us
  Pallas kernels  99.2 us (95%)
  local copies, waits for them, and re-layouts  4 us (4%)
    pallas_call x1, Pallas kernels, on_device(): pl.pallas_call(reduce_kernel, out_shape=(jax.ShapeDtypeStruct((HALF, F),...  50.9 us
    pallas_call x1, Pallas kernels, on_device(): pl.pallas_call(gather_kernel, out_shape=(jax.ShapeDtypeStruct((4, 2, NX,...  34.1 us
    pallas_call x1, Pallas kernels, on_device(): pl.pallas_call(product_kernel, out_shape=jax.ShapeDtypeStruct((UNITS * RB...  14.2 us
    unnamed x2, local copies, waits for them, and re-layouts  2.75 us

profile of v1, /device:TPU:1, one launch (start us, length us, event | category | flops | bytes accessed | tf_op | source)
XLA Modules:
  0.0 103.9 jit_solution(7540570213809831381)
XLA Ops:
  0.6 1.3 %pad.4.perm = s32[8,128]{1,0:T(8,128)} pad(s32[1,8]{1,0:T(1,128)} %bitcast.13, s32[]{:T(128)} %constant.0.clone.1), padding=0_7x0_120 | pad | bytes 4132 | tf_op jit(solution)/shard_map/jit(_pad)/pad | solution.py:413
  1.9 34.1 %gather.1 = (bf16[4,2,4,2,128,128]{5,4,3,2,1,0:T(8,128)(2,1)}, s32[4,8,128]{2,1,0:T(8,128)}) custom-call(bf16[2,4,2,128,128]{4,3,2,1,0:T(8,128)(2,1)} %bitcast.10, s32[8,128]{1,0:T(8,128)} %pad.4.perm), custom_call_target="tpu_custom_call" | custom-call | tf_op jit(solution)/shard_map/gather/pallas_call | solution.py:415
  36.0 14.2 %products.1 = f32[48,256,128]{2,1,0:T(8,128)} custom-call(s32[1,36]{1,0:T(1,128)} %rows.1, s32[1,36]{1,0:T(1,128)} %cols.1, s32[4,8,128]{2,1,0:T(8,128)} %get-tuple-element.6.perms, bf16[32,256,128]{2,1,0:T(8,128)(2,1)} %bitcast.9, bf16[36,256,256]{2,1,0:T(8,128)(2,1)} %bitcast.8), custom_call_target="tpu_custom_call" | custom-call | tf_op jit(solution)/shard_map/products/pallas_call | solution.py:431
  50.2 50.9 %reduce.1 = (bf16[128,128]{1,0:T(8,128)(2,1)}, bf16[128,128]{1,0:T(8,128)(2,1)}) custom-call(f32[6,2,4,2,128,128]{5,4,3,2,1,0:T(8,128)} %bitcast.7), custom_call_target="tpu_custom_call" | custom-call | tf_op jit(solution)/shard_map/reduce/pallas_call | solution.py:441
  101.1 1.4 %copy.9 = bf16[1,128,128]{2,1,0:T(8,128)(2,1)} copy(bf16[1,128,128]{2,1,0:T(8,128)(2,1)} %bitcast.12) | data formatting | bytes 65536
  102.5 1.4 %copy.10 = bf16[1,128,128]{2,1,0:T(8,128)(2,1)} copy(bf16[1,128,128]{2,1,0:T(8,128)(2,1)} %bitcast.11) | data formatting | bytes 65536
